TPU v7x, 128 devices: a whole 4x4x4 slice. The times are simulated.
128 devices in a mesh: row: 16 (over z_lo, x, core), col: 8 (over z_hi, y).
Axes of the slice: x: 4, y: 4, z: 4 (z_hi: 2, z_lo: 2; z = z_hi * 2 + z_lo), core: 2. Of those that a mesh axis runs over, the one named last changes fastest.
Arguments:
- inverse_front: float32 [16384, 16384], P('row', 'col'), may hold values from -0.09375 to 0.09375
- factor: float32 [4096, 1024], P('row'), may hold values from -1.2 to 1.2
- unit_lower: float32 [2, 512, 512], replicated, may hold values from -0.25 to 0.25
- pivot_inverse: float32 [2, 512], replicated, may hold values from 0.5 to 4
- tile_list: int32 [2, 16], replicated, may hold values from 0 to 63, as said below
- tile_valid: int32 [2, 16], replicated, may hold values from 0 to 1, as said below
Outputs:
- inverse_column: float32 [16384, 1024], P('row')
- diagonal_block: float32 [2, 512, 512], replicated
Inputs may be any that keep to these rules, and one draw needn't show every extreme that they name: `tile_list`: each row names 16 different tile rows of the front in increasing order, exactly 1 of them among each aligned group of 4 tile rows, and the last tile row is always among them. `tile_valid`: each row holds at least one 1.
All inputs are finite; a program needn't handle non-finite values.
Results may differ from a plain program's by a relative error of at most 0.0001.
Values sent between devices are 32-bit elements; how exact they have to be, the bound alone decides.
A program may use at most 192 MiB of HBM per device.

v0:
```python
import jax
import jax.numpy as jnp
from jax import lax
from jax.sharding import PartitionSpec as P

B = 256
W = 512
NS = 2
NA = 16


def from_root(block, axis, owner):
    block = jnp.where(lax.axis_index(axis) == owner, block, jnp.zeros_like(block))
    return lax.psum(block, axis)


def inner_left(left, right):
    return lax.dot_general(
        left,
        right,
        (((0,), (0,)), ((), ())),
        precision=lax.Precision.HIGHEST,
        preferred_element_type=jnp.float32,
    )


def shards(inverse_front, factor, unit_lower, pivot_inverse, tile_list, tile_valid):
    row_count = lax.axis_size("row")
    col_count = lax.axis_size("col")
    row_span, col_span = inverse_front.shape
    row_index = lax.axis_index("row")
    col_index = lax.axis_index("col")
    identity = jnp.eye(W, dtype=jnp.float32)
    inverses = [jnp.tril(unit_lower[member], -1) + identity for member in range(NS)]

    def normalize(slab):
        return jnp.concatenate(
            [
                jnp.dot(
                    slab[:, member * W : (member + 1) * W],
                    inverses[member],
                    precision=lax.Precision.HIGHEST,
                    preferred_element_type=jnp.float32,
                )
                for member in range(NS)
            ],
            axis=1,
        )

    normalized = lax.all_gather(normalize(factor), "row", axis=0, tiled=True)
    slot_tiles = normalized.reshape(NA, B, NS, W)

    def place_tiles(first, number):
        global_tile = first + jnp.arange(number, dtype=jnp.int32)
        onehot = (
            (tile_list[:, None, :] == global_tile[None, :, None]) & (tile_valid[:, None, :] > 0)
        ).astype(jnp.float32)
        placed = jnp.einsum("sta,absw->tbsw", onehot, slot_tiles, precision=lax.Precision.HIGHEST)
        return (placed.reshape(number * B, NS * W), jnp.sum(onehot, axis=2))

    row_factor, row_chosen = place_tiles(row_index * (row_span // B), row_span // B)
    col_factor, col_chosen = place_tiles(col_index * (col_span // B), col_span // B)
    row_global = row_index * row_span + jnp.arange(row_span, dtype=jnp.int32)
    col_global = col_index * col_span + jnp.arange(col_span, dtype=jnp.int32)
    lower_part = jnp.where(row_global[:, None] >= col_global[None, :], inverse_front, 0.0)
    lower_prod = jnp.dot(
        lower_part, col_factor, precision=lax.Precision.HIGHEST, preferred_element_type=jnp.float32
    )
    strict = jnp.where(row_global[:, None] > col_global[None, :], inverse_front, 0.0)
    mirror_prod = inner_left(strict, row_factor)
    row_total = lax.psum(lower_prod, "col")
    col_total = lax.psum(mirror_prod, "row")
    grid_ratio = row_count // col_count
    offset = row_index % grid_ratio * row_span
    own_piece = lax.dynamic_slice_in_dim(col_total, offset, row_span, 0)
    mirrored = from_root(own_piece, "col", row_index // grid_ratio)
    keep_rows = jnp.repeat(row_chosen, B, axis=1)
    keep_mask = jnp.repeat(keep_rows.T, W, axis=1)
    column = -(row_total + mirrored) * keep_mask
    base_block = jnp.stack(
        [
            jnp.dot(
                inverses[member].T * pivot_inverse[member][None, :],
                inverses[member],
                precision=lax.Precision.HIGHEST,
                preferred_element_type=jnp.float32,
            )
            for member in range(NS)
        ]
    )
    diag_terms = jnp.stack(
        [
            inner_left(
                row_factor[:, member * W : (member + 1) * W],
                column[:, member * W : (member + 1) * W],
            )
            for member in range(NS)
        ]
    )
    diag_total = lax.psum(diag_terms, "row")
    diagonal_block = base_block - diag_total
    return (column, diagonal_block)


def solution(mesh):
    in_specs = (P("row", "col"), P("row", None), P(), P(), P(), P())
    out_specs = (P("row", None), P())
    return jax.shard_map(shards, mesh=mesh, in_specs=in_specs, out_specs=out_specs, check_vma=False)
```

profile of v0, /device:TPU:1, one launch (start us, length us, event | category | flops | bytes accessed | tf_op | source)
XLA Modules:
  0.0 620.7 jit_solution(13033368712311143179)
XLA Ops:
  7.2 3.3 convolution_bitcast_fusion.1
  10.5 3.3 convolution_bitcast_fusion.2
  15.0 95.2 %all-gather.2.cloned.1.call-done = f32[4096,1024]{0,1:T(8,128)} async-done(((f32[256,1024]{0,1:T(8,128)}), f32[4096,1024]{0,1:T(8,128)}) %all-gather.2.cloned.1.call-update) | async-done | bytes 16777232 | tf_op jit(solution)/shard_map/all_gather | solution.py:50
  110.2 11.0 %copy.23 = f32[128,8,16,256]{3,2,1,0:T(8,128)S(1)} copy(f32[128,8,16,256]{3,1,2,0:T(8,128)} %bitcast.71) | data formatting | bytes 33554432
  121.2 6.5 %fusion.57 = f32[2,256,512,4]{1,3,2,0:T(4,128)S(1)} fusion(f32[16,256,2,512]{1,0,3,2:T(8,128)S(1)} %bitcast.67, s32[2,16]{1,0:T(2,128)S(1)} %copy-done.5, pred[2,16]{1,0:T(4,128)(4,1)S(1)} %broadcast_compare_fusion, s32[4]{0:T(128)S(1)} %iota_add_fusion.3), kind=kOutput, calls=%fused_computation.60 | convolution fusion | flops 201326848 | bytes 20971696 | tf_op jit(solution)/shard_map/sta,absw->tbsw/dot_general | solution.py:58
  128.8 2.0 copy-done.2
  130.8 57.2 %fusion = f32[2048,1024]{1,0:T(8,128)} fusion(f32[1024,1024]{0,1:T(8,128)S(1)} %bitcast.72, f32[1024,2048]{1,0:T(8,128)} %param.6, s32[2048]{0:T(1024)S(1)} %iota_add_fusion, s32[1024]{0:T(1024)S(1)} %iota_add_fusion.1), kind=kOutput, calls=%fused_computation | convolution fusion | flops 25773998080 | bytes 20983808 | tf_op jit(solution)/shard_map/dot_general | solution.py:18
  188.1 20.3 %copy.14 = f32[16,256,2,512]{3,0,1,2:T(8,128)} copy(f32[16,256,2,512]{1,0,3,2:T(8,128)} %bitcast.68) | data formatting | bytes 33554432 | tf_op jit(solution)/shard_map/reshape | solution.py:51
  208.4 11.9 %convolution_bitcast_fusion = f32[8,256,2,512]{3,0,1,2:T(8,128)} fusion(f32[16,256,2,512]{3,0,1,2:T(8,128)} %copy.14, s32[2,16]{1,0:T(2,128)S(1)} %copy-done.5, s32[8]{0:T(128)S(1)} %iota_add_fusion.4, pred[2,16]{1,0:T(4,128)(4,1)S(1)} %broadcast_compare_fusion), kind=kOutput, calls=%fused_computation.14 | convolution fusion | flops 402653696 | bytes 25166016 | tf_op jit(solution)/shard_map/sta,absw->tbsw/dot_general | solution.py:58
  220.4 10.5 %copy.15 = f32[8,256,2,512]{1,0,3,2:T(8,128)} copy(f32[8,256,2,512]{3,0,1,2:T(8,128)} %convolution_bitcast_fusion) | data formatting | bytes 16777216 | tf_op jit(solution)/shard_map/sta,absw->tbsw/transpose | solution.py:58
  230.8 10.9 %copy.24 = f32[128,8,8,256]{3,1,2,0:T(8,128)} copy(f32[128,8,8,256]{3,2,1,0:T(8,128)} %bitcast.69) | data formatting | bytes 16777216
  241.8 87.7 %all-reduce.4.cloned.1.call-done = f32[2048,1024]{1,0:T(8,128)} async-done(((f32[2048,1024]{1,0:T(8,128)}), f32[2048,1024]{1,0:T(8,128)}) %all-reduce.4.cloned.1.call-update) | async-done | bytes 8388624 | tf_op jit(solution)/shard_map/psum | solution.py:72
  329.5 33.9 %select_add_fusion = f32[1024,1024]{1,0:T(8,128)} fusion(f32[2048,1024]{1,0:T(8,128)} %all-reduce.4.cloned.1.call-done, s32[]{:T(128)S(6)} %select_n.43, pred[]{:T(512)S(6)} %eq.40, f32[2048,1024]{0,1:T(8,128)} %bitcast.77, f32[1024,2048]{1,0:T(8,128)} %param.6, s32[2048]{0:T(1024)S(1)} %iota_add_fusion, s32[1024]{0:T(1024)S(1)} %iota_add_fusion.1), kind=kOutput, calls=%fused_computation.7 | convolution fusion | flops 25776095232 | bytes 25178116 | tf_op jit(solution)/shard_map/dot_general | solution.py:66
  363.9 1.4 broadcast_in_dim.33
  365.3 3.0 copy.26
  368.3 106.8 %all-reduce.8.cloned.1.call-done = f32[1024,1024]{1,0:T(8,128)} async-done(((f32[1024,1024]{1,0:T(8,128)}), f32[1024,1024]{1,0:T(8,128)}) %all-reduce.8.cloned.1.call-update) | async-done | bytes 4194320 | tf_op jit(solution)/shard_map/psum | solution.py:71
  475.1 4.6 negate_multiply_fusion
  479.8 3.5 fusion.35
  483.3 3.5 fusion.30
  486.8 1.5 pad_maximum_fusion
  489.2 2.3 fusion.27
  491.5 3.3 fusion.24
  494.8 115.6 %all-reduce.6.cloned.1.call-done = f32[2,512,512]{2,1,0:T(8,128)} async-done(((f32[2,512,512]{2,1,0:T(8,128)}), f32[2,512,512]{2,1,0:T(8,128)}) %all-reduce.6.cloned.1.call-update) | async-done | bytes 2097168 | tf_op jit(solution)/shard_map/psum | solution.py:100
  610.4 3.7 maximum_subtract_fusion
  (35 shorter events, 3.7 us)
Async XLA Ops:
  7.2 7.8 %copy-start.7 = (s32[2,16]{1,0:T(2,128)S(1)}, s32[2,16]{1,0:T(2,128)}, u32[]{:S(2)}) copy-start(s32[2,16]{1,0:T(2,128)} %param.11) | copy-start | bytes 388
  7.2 103.1 %all-gather.2.cloned.1.call-start = ((), (), s32[]{:S(2)}) async-start(), calls=%async_computation | async-start | bytes 17825792 | tf_op jit(solution)/shard_map/all_gather | solution.py:50
  14.9 314.6 %all-reduce.4.cloned.1.call-start = ((), (), s32[]{:S(2)}) async-start(), calls=%async_computation.1 | async-start | bytes 16777216 | tf_op jit(solution)/shard_map/psum | solution.py:72
  110.2 11.0 %copy-start.5 = (s32[2,16]{1,0:T(2,128)S(1)}, s32[2,16]{1,0:T(2,128)}, u32[]{:S(2)}) copy-start(s32[2,16]{1,0:T(2,128)} %param.10) | copy-start | bytes 388
  121.2 6.5 %copy-start = (f32[128,8,16,256]{3,2,1,0:T(8,128)}, f32[128,8,16,256]{3,2,1,0:T(8,128)S(1)}, u32[]{:S(2)}) copy-start(f32[128,8,16,256]{3,2,1,0:T(8,128)S(1)} %copy.23) | copy-start | bytes 50331652
  128.8 2.1 copy-start.2
  188.0 287.1 %all-reduce.8.cloned.1.call-start = ((), (), s32[]{:S(2)}) async-start(), calls=%async_computation.3 | async-start | bytes 8388608 | tf_op jit(solution)/shard_map/psum | solution.py:71
  363.4 247.0 %all-reduce.6.cloned.1.call-start = ((), (), s32[]{:S(2)}) async-start(), calls=%async_computation.2 | async-start | bytes 4194304 | tf_op jit(solution)/shard_map/psum | solution.py:100
  475.1 4.6 copy-start.3
  479.8 7.0 %copy-start.1 = (f32[1024,1024]{1,0:T(8,128)}, f32[1024,1024]{1,0:T(8,128)S(1)}, u32[]{:S(2)}) copy-start(f32[1024,1024]{1,0:T(8,128)S(1)} %negate_multiply_fusion) | copy-start | bytes 12582916
  486.8 1.5 copy-start.6
  486.8 2.4 copy-start.4
Sparse Core Ops, SparseCore 0:
  15.0 95.2 all-gather.1
  188.1 141.3 all-reduce.3
  363.5 111.5 all-reduce.7
  488.5 121.8 all-reduce.5
where the time goes:
time: 629 us; the launch traced here: 621 us
  waiting for transfers between devices  405 us (64%)
  matrix products  129 us (21%)
  local copies, waits for them, and re-layouts  61.2 us (10%)
  between operations  14.2 us (2%)
  other arithmetic  10.9 us (2%)
    psum x1, waiting for transfers between devices, shards(): diag_total = lax.psum(diag_terms, 'row')  116 us
    psum x1, waiting for transfers between devices, shards(): row_total = lax.psum(lower_prod, 'col')  107 us
    all_gather x1, waiting for transfers between devices, shards(): normalized = lax.all_gather(normalize(factor), 'row', axis=0, tiled=True)  95.2 us
    psum x1, waiting for transfers between devices, shards(): col_total = lax.psum(mirror_prod, 'row')  87.7 us
    dot_general x3, matrix products, inner_left(): lax.dot_general(left, right, (((0,), (0,)), ((), ())), precision=lax.Prec...  64.2 us
    dot_general x1, matrix products, shards(): jnp.dot(lower_part, col_factor, precision=lax.Precision.HIGHEST, preferre...  33.9 us
    unnamed x20, local copies, waits for them, and re-layouts  28.9 us
    reshape x1, local copies, waits for them, and re-layouts, shards(): slot_tiles = normalized.reshape(NA, B, NS, W)  20.3 us
  transfers between devices with their start and end apart: 4, of which 4 were waited for; matrix products, arithmetic and copies ran while one was open for 10% of the time, Pallas kernels for 0%

commit v1 on v0

--- a/solution.py
+++ b/solution.py
@@ -97,7 +97,7 @@
             for member in range(NS)
         ]
     )
-    diag_total = lax.psum(diag_terms, "row")
+    diag_total = jnp.sum(lax.all_gather(diag_terms, "row"), axis=0)
     diagonal_block = base_block - diag_total
     return (column, diagonal_block)
 

time: 629 us -> 689 us (1.095)
  waiting for transfers between devices: 405 us -> 453 us
  other arithmetic: 10.9 us -> 23.1 us
    all_gather x0 -> x1, waiting for transfers between devices: none -> 163 us  [shards(): diag_total = jnp.sum(lax.all_gather(diag_terms, 'row'), axis=0)]
    psum x1 -> x0, waiting for transfers between devices: 116 us -> none  [shards(): diag_total = lax.psum(diag_terms, 'row')]
    reduce_sum x0 -> x1, other arithmetic: none -> 12.7 us  [shards(): diag_total = jnp.sum(lax.all_gather(diag_terms, 'row'), axis=0)]
  transfers between devices with their start and end apart: 4 -> 4, of which waited for: 4 -> 4; matrix products, arithmetic and copies ran while one was open for 10% -> 9% of each run, Pallas kernels for 0% -> 0%
where the time goes in v1:
time: 689 us; the launch traced here: 681 us
  waiting for transfers between devices  453 us (66%)
  matrix products  129 us (19%)
  local copies, waits for them, and re-layouts  61.2 us (9%)
  other arithmetic  23.1 us (3%)
  between operations  14.2 us (2%)
    all_gather x1, waiting for transfers between devices, shards(): diag_total = jnp.sum(lax.all_gather(diag_terms, 'row'), axis=0)  163 us
    psum x1, waiting for transfers between devices, shards(): row_total = lax.psum(lower_prod, 'col')  107 us
    all_gather x1, waiting for transfers between devices, shards(): normalized = lax.all_gather(normalize(factor), 'row', axis=0, tiled=True)  95.2 us
    psum x1, waiting for transfers between devices, shards(): col_total = lax.psum(mirror_prod, 'row')  87.7 us
    dot_general x3, matrix products, inner_left(): lax.dot_general(left, right, (((0,), (0,)), ((), ())), precision=lax.Prec...  64.2 us
    dot_general x1, matrix products, shards(): jnp.dot(lower_part, col_factor, precision=lax.Precision.HIGHEST, preferre...  33.9 us
    unnamed x20, local copies, waits for them, and re-layouts  28.9 us
    reshape x1, local copies, waits for them, and re-layouts, shards(): slot_tiles = normalized.reshape(NA, B, NS, W)  20.3 us
  transfers between devices with their start and end apart: 4, of which 4 were waited for; matrix products, arithmetic and copies ran while one was open for 9% of the time, Pallas kernels for 0%

profile of v1, /device:TPU:1, one launch (start us, length us, event | category | flops | bytes accessed | tf_op | source)
XLA Modules:
  0.0 680.8 jit_solution(1517668559472173064)
XLA Ops:
  7.2 3.3 convolution_bitcast_fusion.1
  10.5 3.3 convolution_bitcast_fusion.2
  15.0 95.2 %all-gather.4.cloned.1.call-done = f32[4096,1024]{0,1:T(8,128)} async-done(((f32[256,1024]{0,1:T(8,128)}), f32[4096,1024]{0,1:T(8,128)}) %all-gather.4.cloned.1.call-update) | async-done | bytes 16777232 | tf_op jit(solution)/shard_map/all_gather | solution.py:50
  110.2 11.0 %copy.23 = f32[128,8,16,256]{3,2,1,0:T(8,128)S(1)} copy(f32[128,8,16,256]{3,1,2,0:T(8,128)} %bitcast.73) | data formatting | bytes 33554432
  121.2 6.5 fusion.57
  128.8 2.0 copy-done.2
  130.8 57.2 %fusion = f32[2048,1024]{1,0:T(8,128)} fusion(f32[1024,1024]{0,1:T(8,128)S(1)} %bitcast.74, f32[1024,2048]{1,0:T(8,128)} %param.6, s32[2048]{0:T(1024)S(1)} %iota_add_fusion, s32[1024]{0:T(1024)S(1)} %iota_add_fusion.1), kind=kOutput, calls=%fused_computation | convolution fusion | flops 25773998080 | bytes 20983808 | tf_op jit(solution)/shard_map/dot_general | solution.py:18
  188.1 20.3 %copy.14 = f32[16,256,2,512]{3,0,1,2:T(8,128)} copy(f32[16,256,2,512]{1,0,3,2:T(8,128)} %bitcast.69) | data formatting | bytes 33554432 | tf_op jit(solution)/shard_map/reshape | solution.py:51
  208.4 11.9 %convolution_bitcast_fusion = f32[8,256,2,512]{3,0,1,2:T(8,128)} fusion(f32[16,256,2,512]{3,0,1,2:T(8,128)} %copy.14, s32[2,16]{1,0:T(2,128)S(1)} %copy-done.5, s32[8]{0:T(128)S(1)} %iota_add_fusion.4, pred[2,16]{1,0:T(4,128)(4,1)S(1)} %broadcast_compare_fusion), kind=kOutput, calls=%fused_computation.14 | convolution fusion | flops 402653696 | bytes 25166016 | tf_op jit(solution)/shard_map/sta,absw->tbsw/dot_general | solution.py:58
  220.4 10.5 %copy.15 = f32[8,256,2,512]{1,0,3,2:T(8,128)} copy(f32[8,256,2,512]{3,0,1,2:T(8,128)} %convolution_bitcast_fusion) | data formatting | bytes 16777216 | tf_op jit(solution)/shard_map/sta,absw->tbsw/transpose | solution.py:58
  230.8 10.9 %copy.24 = f32[128,8,8,256]{3,1,2,0:T(8,128)} copy(f32[128,8,8,256]{3,2,1,0:T(8,128)} %bitcast.71) | data formatting | bytes 16777216
  241.8 87.7 %all-reduce.3.cloned.1.call-done = f32[2048,1024]{1,0:T(8,128)} async-done(((f32[2048,1024]{1,0:T(8,128)}), f32[2048,1024]{1,0:T(8,128)}) %all-reduce.3.cloned.1.call-update) | async-done | bytes 8388624 | tf_op jit(solution)/shard_map/psum | solution.py:72
  329.5 33.9 %select_add_fusion = f32[1024,1024]{1,0:T(8,128)} fusion(f32[2048,1024]{1,0:T(8,128)} %all-reduce.3.cloned.1.call-done, s32[]{:T(128)S(6)} %select_n.43, pred[]{:T(512)S(6)} %eq.40, f32[2048,1024]{0,1:T(8,128)} %bitcast.79, f32[1024,2048]{1,0:T(8,128)} %param.6, s32[2048]{0:T(1024)S(1)} %iota_add_fusion, s32[1024]{0:T(1024)S(1)} %iota_add_fusion.1), kind=kOutput, calls=%fused_computation.7 | convolution fusion | flops 25776095232 | bytes 25178116 | tf_op jit(solution)/shard_map/dot_general | solution.py:66
  365.3 3.0 copy.26
  368.3 106.8 %all-reduce.5.cloned.1.call-done = f32[1024,1024]{1,0:T(8,128)} async-done(((f32[1024,1024]{1,0:T(8,128)}), f32[1024,1024]{1,0:T(8,128)}) %all-reduce.5.cloned.1.call-update) | async-done | bytes 4194320 | tf_op jit(solution)/shard_map/psum | solution.py:71
  475.1 4.6 negate_multiply_fusion
  479.8 3.5 fusion.35
  483.3 3.5 fusion.30
  486.8 1.5 pad_maximum_fusion
  489.2 2.3 fusion.27
  491.5 3.3 fusion.24
  494.8 163.5 %all-gather.6.cloned.1.call-done = f32[32,512,512]{2,1,0:T(8,128)} async-done(((f32[2,512,512]{2,1,0:T(8,128)}), f32[32,512,512]{2,1,0:T(8,128)}) %all-gather.6.cloned.1.call-update) | async-done | bytes 33554448 | tf_op jit(solution)/shard_map/all_gather | solution.py:100
  658.3 12.7 %reduce_sum.19 = f32[2,512,512]{2,1,0:T(8,128)S(1)} reduce(f32[16,2,512,512]{3,2,1,0:T(8,128)} %bitcast.70, f32[]{:T(128)} %constant.45.clone.1), dimensions={0}, to_apply=%region_4.5 | reduce | flops 7864320 | bytes 35651588 | tf_op jit(solution)/shard_map/reduce_sum | solution.py:100
  671.0 3.0 maximum_subtract_fusion
  (36 shorter events, 5.1 us)
Async XLA Ops:
  7.2 7.8 %copy-start.7 = (s32[2,16]{1,0:T(2,128)S(1)}, s32[2,16]{1,0:T(2,128)}, u32[]{:S(2)}) copy-start(s32[2,16]{1,0:T(2,128)} %param.11) | copy-start | bytes 388
  7.2 103.1 %all-gather.4.cloned.1.call-start = ((), (), s32[]{:S(2)}) async-start(), calls=%async_computation | async-start | bytes 17825792 | tf_op jit(solution)/shard_map/all_gather | solution.py:50
  14.9 314.6 %all-reduce.3.cloned.1.call-start = ((), (), s32[]{:S(2)}) async-start(), calls=%async_computation.1 | async-start | bytes 16777216 | tf_op jit(solution)/shard_map/psum | solution.py:72
  110.2 11.0 %copy-start.5 = (s32[2,16]{1,0:T(2,128)S(1)}, s32[2,16]{1,0:T(2,128)}, u32[]{:S(2)}) copy-start(s32[2,16]{1,0:T(2,128)} %param.10) | copy-start | bytes 388
  121.2 6.5 copy-start
  128.8 2.1 copy-start.2
  188.0 287.1 %all-reduce.5.cloned.1.call-start = ((), (), s32[]{:S(2)}) async-start(), calls=%async_computation.3 | async-start | bytes 8388608 | tf_op jit(solution)/shard_map/psum | solution.py:71
  363.4 294.9 %all-gather.6.cloned.1.call-start = ((), (), s32[]{:S(2)}) async-start(), calls=%async_computation.2 | async-start | bytes 35651584 | tf_op jit(solution)/shard_map/all_gather | solution.py:100
  475.1 4.6 copy-start.3
  479.8 7.0 %copy-start.1 = (f32[1024,1024]{1,0:T(8,128)}, f32[1024,1024]{1,0:T(8,128)S(1)}, u32[]{:S(2)}) copy-start(f32[1024,1024]{1,0:T(8,128)S(1)} %negate_multiply_fusion) | copy-start | bytes 12582916
  486.8 1.5 copy-start.6
  486.8 2.4 copy-start.4
Sparse Core Ops, SparseCore 0:
  15.0 95.2 all-gather.3
  188.1 141.3 all-reduce.2
  363.5 111.5 all-reduce.4
  488.5 169.7 all-gather.5
